TPU v7x, 512 devices: a whole 4x8x8 slice. The times are simulated.
512 devices in a mesh: gz: 64 (over y, x, core), gy: 8 (over z).
Axes of the slice: x: 4, y: 8, z: 8, core: 2. Of those that a mesh axis runs over, the one named last changes fastest.
Arguments:
- scalar: float32 [128, 512, 1024], P('gz', 'gy'), as said below
- bin_index: int32 [128, 512, 1024], P('gz', 'gy'), may hold values from 0 to 255, as said below
- color_table: bfloat16 [3, 257], replicated, may hold values from 0.099609375 to 1
- opacity_table: bfloat16 [257], replicated, may hold values from 0.00049972534 to 0.019897461
- light_dir: float32 [3], replicated, may hold values from -4 to 4
- view_order: int32 [64], replicated, may hold values from 0 to 63, each once
Outputs:
- image_rgba: float32 [4, 8, 64, 1024], P(None, 'gy', 'gz')
Inputs may be any that keep to these rules, and one draw needn't show every extreme that they name: bin_index is the floor of 256 scalar in every cell, except that fraction may reach 1. scalar lies between bin_index / 256 and (bin_index + 1) / 256. `view_order`: each brick position appears once.
All inputs are finite; a program needn't handle non-finite values.
Results may differ from a plain program's by a relative error of at most 0.0003.
Values sent between devices are 32-bit elements; how exact they have to be, the bound alone decides.
A program may use at most 64 MiB of HBM per device.

v0:
```python
import jax
import jax.numpy as jnp
from jax import lax
from jax.sharding import PartitionSpec as P


def extended(x, sides, width):
    for axis, dim in sides:
        devices, length = (lax.axis_size(axis), x.shape[dim])
        up = [(i, (i + 1) % devices) for i in range(devices - 1)]
        down = [(j, i) for i, j in up]
        last = lax.slice_in_dim(x, length - width, length, axis=dim)
        initial = lax.slice_in_dim(x, 0, width, axis=dim)
        before = lax.ppermute(last, axis, up)
        after = lax.ppermute(initial, axis, down)
        x = jnp.concatenate([before, x, after], axis=dim)
    return x


def shading_from(field, row_padded, light_dir):
    next_slice = jnp.concatenate([field[1:], field[-1:]], axis=0)
    behind = jnp.concatenate([field[:1], field[:-1]], axis=0)
    grad_depth = next_slice - behind
    grad_rows = row_padded[:, 2:] - row_padded[:, :-2]
    col_padded = jnp.pad(field, ((0, 0), (0, 0), (1, 1)))
    grad_cols = col_padded[:, :, 2:] - col_padded[:, :, :-2]
    facing = grad_depth * light_dir[0] + grad_rows * light_dir[1] + grad_cols * light_dir[2]
    squared = grad_depth * grad_depth + grad_rows * grad_rows + grad_cols * grad_cols
    return 0.25 + 0.75 * facing * facing / (squared + 1.0)


def blend_emission(lower, upper, fraction, shading):
    blended = (1.0 - fraction) * lower + fraction * upper
    opacity = blended[3]
    emitted = opacity * shading * blended[:3]
    return (emitted, jnp.log1p(-opacity))


def shards(scalar, bin_index, color_table, opacity_table, light_dir, view_order):
    depth_count, row_count, col_count = scalar.shape
    bricks = lax.axis_size("gz")
    tile_rows = row_count // bricks
    band_rows = 16
    band_count = row_count // band_rows
    block_count = depth_count * band_count
    block_cells = band_rows * col_count
    bin_count = color_table.shape[1] - 1
    stacked = jnp.concatenate(
        [
            color_table[:, :-1],
            opacity_table[None, :-1],
            color_table[:, 1:],
            opacity_table[None, 1:],
        ],
        axis=0,
    )
    fraction = scalar * bin_count - bin_index.astype(jnp.float32)
    row_padded = extended(scalar, (("gy", 1),), 1)
    shading = shading_from(scalar, row_padded, light_dir)
    levels = lax.broadcasted_iota(jnp.int32, (bin_count, 1), 0)

    def lookup(pieces):
        codes_block, fraction_block, shading_block = pieces
        onehot = (levels == codes_block[None, :]).astype(jnp.bfloat16)
        looked_up = jnp.dot(stacked, onehot, preferred_element_type=jnp.float32)
        return blend_emission(looked_up[:4], looked_up[4:], fraction_block, shading_block)

    def as_blocks(values):
        return values.reshape(block_count, block_cells)

    emitted, log_keep = lax.map(
        lookup, (as_blocks(bin_index), as_blocks(fraction), as_blocks(shading))
    )
    emitted = emitted.reshape(depth_count, band_count, 3, block_cells)
    log_keep = log_keep.reshape(depth_count, band_count, block_cells)
    passed = jnp.cumsum(log_keep, axis=0) - log_keep
    brick_color = jnp.sum(emitted * jnp.exp(passed)[:, :, None, :], axis=0)
    brick_keep = jnp.sum(log_keep, axis=0)
    color_part = jnp.transpose(brick_color, (1, 0, 2)).reshape(3, bricks, tile_rows, col_count)
    keep_part = brick_keep.reshape(1, bricks, tile_rows, col_count)
    earlier = (view_order[None, :] < view_order[:, None]).astype(jnp.float32)
    keep_in = lax.all_to_all(keep_part, "gz", split_axis=1, concat_axis=1, tiled=True)
    before = jnp.einsum("ji,cirw->cjrw", earlier, keep_in, precision=lax.Precision.HIGHEST)
    own_before = lax.all_to_all(before, "gz", split_axis=1, concat_axis=1, tiled=True)
    weighted = color_part * jnp.exp(own_before)
    color_sum = lax.psum_scatter(weighted, "gz", scatter_dimension=1, tiled=True)
    coverage = 1.0 - jnp.exp(jnp.sum(keep_in, axis=1, keepdims=True))
    return jnp.concatenate([color_sum, coverage], axis=0)


def solution(mesh):
    in_specs = (P("gz", "gy", None), P("gz", "gy", None), P(), P(), P(), P())
    out_specs = P(None, "gy", "gz", None)
    return jax.shard_map(shards, mesh=mesh, in_specs=in_specs, out_specs=out_specs, check_vma=False)
```

profile of v0, /device:TPU:1, one launch (start us, length us, event | category | flops | bytes accessed | tf_op | source)
XLA Modules:
  0.0 328.4 jit_solution(4786999260991093714)
XLA Ops:
  6.5 1.0 fusion.17
  7.5 1.3 collective-permute-start
  8.8 5.4 %collective-permute-start.1 = (f32[2,1,1024]{2,1,0:T(1,128)S(1)}, f32[2,1,1024]{2,1,0:T(1,128)S(1)}, u32[]{:S(2)}, u32[]{:S(2)}) collective-permute-start(f32[2,1,1024]{2,1,0:T(1,128)S(1)} %get-tuple-element.89), channel_id=1, source_target_pairs={{0,1},{1,2},{2,3},{3,4},{4,5},{5,6},{6,7},{8,9},{9,10},{10,11},{11... | collective-permute-start | bytes 24584 | tf_op jit(solution)/shard_map/ppermute | solution.py:14
  14.3 1.8 fusion.16
  16.1 1.4 fusion.20
  17.5 0.8 fusion.18
  18.3 0.8 fusion.19
  19.2 1.9 reshape.71
  21.1 4.4 %fusion.9 = (f32[2,64,1024]{2,1,0:T(8,128)}, f32[2,64,1024]{2,1,0:T(8,128)}) fusion(f32[2,64,1024]{2,1,0:T(8,128)S(1)} %copy-done, f32[2,1,1024]{2,1,0:T(1,128)S(1)} %collective-permute-done.1, f32[2,1,1024]{2,1,0:T(1,128)S(1)} %collective-permute-done, f32[1,64,1024]{2,1,0:T(8,128)} %get-tuple-element.87, f32[1,64,1024]{2,1,0:T(8,128)S(1)} %get-tuple-element.86, ...), kind=kLoop, calls=%fused_computation.24 | loop fusion | flops 3276800 | bytes 2637836 | tf_op jit(solution)/shard_map/add | solution.py:29
  25.5 1.1 reshape.70
  26.6 1.1 reshape.72
  27.8 49.3 %while.13 = (s32[]{:T(128)}, f32[8,3,16384]{2,1,0:T(4,128)S(1)}, f32[8,16384]{1,0:T(8,128)}, f32[8,16384]{1,0:T(8,128)S(1)}, s32[8,16384]{1,0:T(8,128)}, /*index...) while((s32[]{:T(128)}, f32[8,3,16384]{2,1,0:T(4,128)S(1)}, ...), condition=%wide.region_1.2_spmd.clone, body=%wide.region_0.1_spmd.clone.sunk | while | flops 71598080 | bytes 2822257 | solution.py:71
  27.8 1.1 constant_dynamic-slice_fusion.5
  28.9 2.6 convolution_bitcast_fusion.3
  32.0 1.9 dynamic_update_slice.14
  34.0 1.1 constant_dynamic-slice_fusion.5
  35.1 2.6 convolution_bitcast_fusion.3
  38.2 1.9 dynamic_update_slice.14
  40.1 1.1 constant_dynamic-slice_fusion.5
  41.2 2.6 convolution_bitcast_fusion.3
  44.3 1.9 dynamic_update_slice.14
  46.3 1.1 constant_dynamic-slice_fusion.5
  47.4 2.6 convolution_bitcast_fusion.3
  50.5 1.9 dynamic_update_slice.14
  52.5 1.1 constant_dynamic-slice_fusion.5
  53.5 2.6 convolution_bitcast_fusion.3
  56.7 1.9 dynamic_update_slice.14
  58.6 1.1 constant_dynamic-slice_fusion.5
  59.7 2.6 convolution_bitcast_fusion.3
  62.8 1.9 dynamic_update_slice.14
  64.8 1.1 constant_dynamic-slice_fusion.5
  65.9 2.6 convolution_bitcast_fusion.3
  69.0 1.9 dynamic_update_slice.14
  70.9 1.1 constant_dynamic-slice_fusion.5
  72.0 2.6 convolution_bitcast_fusion.3
  75.2 1.9 dynamic_update_slice.14
  77.1 1.2 reduce_window_sum.13
  78.9 23.9 %all_to_all.10 = f32[1,64,1,1024]{3,2,0,1:T(1,128)S(1)} all-to-all(f32[1,64,1,1024]{3,2,0,1:T(1,128)S(1)} %reshape.75), channel_id=1, replica_groups=mesh['gz'=64,'gy'=8] {'gz'}, dimensions={1} | all-to-all | bytes 524288 | tf_op jit(solution)/shard_map/all_to_all | solution.py:82
  103.1 1.0 copy.7
  104.1 5.1 %all-to-all-start.1 = ((f32[1,64,1,1024]{3,2,0,1:T(1,128)}), f32[1,64,1,1024]{3,2,0,1:T(1,128)}, u32[]{:S(2)}, u32[]{:S(2)}) async-start(f32[1,64,1,1024]{3,2,0,1:T(1,128)} %copy.7), calls=%async_computation.1 | async-start | bytes 524288 | tf_op jit(solution)/shard_map/all_to_all | solution.py:84
  109.4 1.1 multiply_reduce_fusion
  110.5 11.8 %all-to-all-done.1 = f32[1,64,1,1024]{3,2,0,1:T(1,128)} async-done(((f32[1,64,1,1024]{3,2,0,1:T(1,128)}), f32[1,64,1,1024]{3,2,0,1:T(1,128)}, u32[]{:S(2)}, u32[]{:S(2)}) %all-to-all-start.1) | async-done | bytes 262176 | tf_op jit(solution)/shard_map/all_to_all | solution.py:84
  122.3 1.2 exp.23
  123.6 1.3 broadcast_multiply_fusion
  124.9 1.3 dynamic-slice
  126.4 193.2 %all-reduce.4.cloned.1.call-done = f32[3,64,1,1024]{3,0,2,1:T(4,128)} async-done(((f32[3,64,1,1024]{3,0,2,1:T(4,128)}), f32[3,64,1,1024]{3,0,2,1:T(4,128)}) %all-reduce.4.cloned.1.call-update) | async-done | bytes 786448
  319.5 1.4 constant_dynamic-slice_fusion.2
  320.9 0.6 copy.8
  (55 shorter events, 5.8 us)
Async XLA Ops:
  6.5 14.6 %copy-start = (f32[2,64,1024]{2,1,0:T(8,128)S(1)}, f32[2,64,1024]{2,1,0:T(8,128)}, u32[]{:S(2)}) copy-start(f32[2,64,1024]{2,1,0:T(8,128)} %param.8) | copy-start | bytes 1572868
  6.5 14.6 %copy-start.1 = (s32[2,64,1024]{2,1,0:T(8,128)S(1)}, s32[2,64,1024]{2,1,0:T(8,128)}, u32[]{:S(2)}) copy-start(s32[2,64,1024]{2,1,0:T(8,128)} %param.9) | copy-start | bytes 1572868
  7.5 13.6 %collective-permute-start = (f32[2,1,1024]{2,1,0:T(1,128)S(1)}, f32[2,1,1024]{2,1,0:T(1,128)S(1)}, u32[]{:S(2)}, u32[]{:S(2)}) collective-permute-start(f32[2,1,1024]{2,1,0:T(1,128)S(1)} %get-tuple-element.88), channel_id=1, source_target_pairs={{1,0},{2,1},{3,2},{4,3},{5,4},{6,5},{7,6},{9,8},{10,9},{11,10},{12... | collective-permute-start | bytes 24584 | tf_op jit(solution)/shard_map/ppermute | solution.py:15
  8.8 12.3 %collective-permute-start.1 = (f32[2,1,1024]{2,1,0:T(1,128)S(1)}, f32[2,1,1024]{2,1,0:T(1,128)S(1)}, u32[]{:S(2)}, u32[]{:S(2)}) collective-permute-start(f32[2,1,1024]{2,1,0:T(1,128)S(1)} %get-tuple-element.89), channel_id=1, source_target_pairs={{0,1},{1,2},{2,3},{3,4},{4,5},{5,6},{6,7},{8,9},{9,10},{10,11},{11... | collective-permute-start | bytes 24584 | tf_op jit(solution)/shard_map/ppermute | solution.py:14
  77.1 25.7 %copy-start.2 = (s32[64]{0:T(128)S(1)}, s32[64]{0:T(128)}, u32[]{:S(2)}) copy-start(s32[64]{0:T(128)} %param.13) | copy-start | bytes 772
  104.1 18.2 %all-to-all-start.1 = ((f32[1,64,1,1024]{3,2,0,1:T(1,128)}), f32[1,64,1,1024]{3,2,0,1:T(1,128)}, u32[]{:S(2)}, u32[]{:S(2)}) async-start(f32[1,64,1,1024]{3,2,0,1:T(1,128)} %copy.7), calls=%async_computation.1 | async-start | bytes 524288 | tf_op jit(solution)/shard_map/all_to_all | solution.py:84
  109.2 210.3 %all-reduce.4.cloned.1.call-start = ((), (), s32[]{:S(2)}) async-start(), calls=%async_computation.2 | async-start | bytes 2097152
Sparse Core Ops, SparseCore 0:
  125.0 194.4 all-reduce.3
where the time goes:
time: 330 us; the launch traced here: 328 us
  waiting for transfers between devices  205 us (62%)
  local copies, waits for them, and re-layouts  41.4 us (13%)
  blocking collectives  23.9 us (7%)
  matrix products  20.7 us (6%)
  between operations  13.5 us (4%)
  starting transfers between devices  11.9 us (4%)
  other arithmetic  11.7 us (4%)
    unnamed x2, waiting for transfers between devices  193 us
    all_to_all x1, blocking collectives, shards(): lax.all_to_all(keep_part, 'gz', split_axis=1, concat_axis=1, tiled=True)  23.9 us
    dot_general x8, matrix products, lookup(): looked_up = jnp.dot(stacked, onehot, preferred_element_type=jnp.float32)  20.4 us
    dynamic_update_slice x8, local copies, waits for them, and re-layouts, shards(): lax.map(lookup, (as_blocks(bin_index), as_blocks(fraction), as_blocks(sha...  15.6 us
    all_to_all x1, waiting for transfers between devices, shards(): lax.all_to_all(before, 'gz', split_axis=1, concat_axis=1, tiled=True)  11.8 us
    dynamic_slice x8, local copies, waits for them, and re-layouts, shards(): lax.map(lookup, (as_blocks(bin_index), as_blocks(fraction), as_blocks(sha...  8.71 us
  transfers between devices with their start and end apart: 4, of which 2 were waited for; matrix products, arithmetic and copies ran while one was open for 3% of the time, Pallas kernels for 0%

commit v1 on v0

v1 whole, which is shorter than its diff:
```python
import jax
import jax.numpy as jnp
from jax import lax
from jax.experimental import pallas as pl
from jax.experimental.pallas import tpu as pltpu
from jax.sharding import PartitionSpec as P

MESH = pl.DeviceIdType.MESH
GY, GJ, GZ = 8, 8, 8
ROWS = 8
MSG = (ROWS + 2) * 8


def remote(src, dst, send_sem, recv_sem, device):
    return pltpu.make_async_remote_copy(
        src_ref=src, dst_ref=dst, send_sem=send_sem, recv_sem=recv_sem, device_id=device, device_id_type=MESH
    )


def kernel(
    x_ref, tab_ref, light_ref, order_ref, out_ref,
    buf, recv, stage, comp, tabs, ord_v, ord_s,
    ys_sem, yr_sem, zs_sem, zr_sem, xs_sem, xr_sem, o_sem,
):
    me, g = lax.axis_index("gz"), lax.axis_index("gy")
    y, j = me // GJ, me % GJ

    def y_peer(d):
        return (((y + d) % GY) * GJ + j, g)

    def x_peer(d):
        return (y * GJ + (j + d) % GJ, g)

    barrier = pltpu.get_barrier_semaphore()
    for d in range(1, 8):
        pl.semaphore_signal(barrier, inc=1, device_id=y_peer(d), device_id_type=MESH)
        pl.semaphore_signal(barrier, inc=1, device_id=x_peer(d), device_id_type=MESH)

    @pl.when(g > 0)
    def _():
        pl.semaphore_signal(barrier, inc=1, device_id=(me, g - 1), device_id_type=MESH)

    @pl.when(g < GZ - 1)
    def _():
        pl.semaphore_signal(barrier, inc=1, device_id=(me, g + 1), device_id_type=MESH)

    for k in range(2):
        for t in range(8):
            for a in range(8):
                buf[k, pl.ds(8 + 64 * t + a, 8, stride=8), :] = x_ref[k, 8 * t : 8 * t + 8, 128 * a : 128 * a + 128]

    @pl.when(g == 0)
    def _():
        buf[:, 0:8, :] = jnp.zeros((2, 8, 128), jnp.float32)

    @pl.when(g == GZ - 1)
    def _():
        buf[:, 520:528, :] = jnp.zeros((2, 8, 128), jnp.float32)

    for i in range(16):
        tabs[i] = jnp.broadcast_to(tab_ref[i : i + 1, :], (8, 128))

    lane = lax.broadcasted_iota(jnp.int32, (8, 128), 1)
    sub = lax.broadcasted_iota(jnp.int32, (8, 128), 0)
    inverse = jnp.zeros((8, 128), jnp.int32)
    for b in range(64):
        inverse = jnp.where(lane == order_ref[b], b, inverse)
    ord_v[...] = inverse
    order_copy = pltpu.make_async_copy(ord_v, ord_s, o_sem)
    order_copy.start()

    pl.semaphore_wait(barrier, 14 + jnp.where(g > 0, 1, 0) + jnp.where(g < GZ - 1, 1, 0))

    down = remote(buf.at[:, pl.ds(512, 8)], buf.at[:, pl.ds(0, 8)], zs_sem.at[0], zr_sem.at[0], (me, (g + 1) % GZ))
    up = remote(buf.at[:, pl.ds(8, 8)], buf.at[:, pl.ds(520, 8)], zs_sem.at[1], zr_sem.at[1], (me, (g + GZ - 1) % GZ))

    @pl.when(g < GZ - 1)
    def _():
        down.start()

    @pl.when(g > 0)
    def _():
        up.start()

    def y_copy(d):
        t = (y + d) % GY
        return remote(buf.at[:, pl.ds(pl.multiple_of(64 * t, 64), MSG)], recv.at[d], ys_sem.at[d], yr_sem.at[d], y_peer(d))

    order = (1, 7, 2, 6, 3, 5, 4)
    for d in order:
        t = (y + d) % GY

        @pl.when((t > 0) & (t < GY - 1))
        def _():
            y_copy(d).start()

    @pl.when(g > 0)
    def _():
        down.wait_recv()

    @pl.when(g < GZ - 1)
    def _():
        up.wait_recv()

    for d in order:
        t = (y + d) % GY

        @pl.when((t == 0) | (t == GY - 1))
        def _():
            y_copy(d).start()

    l0, l1, l2 = light_ref[0], light_ref[1], light_ref[2]

    def shade(s, up_row, down_row, grad_depth):
        a = pltpu.roll(s, 127, 1)
        right = jnp.where(lane == 127, jnp.where(sub == 7, 0.0, pltpu.roll(a, 7, 0)), a)
        b = pltpu.roll(s, 1, 1)
        left = jnp.where(lane == 0, jnp.where(sub == 0, 0.0, pltpu.roll(b, 1, 0)), b)
        grad_cols = right - left
        grad_rows = down_row - up_row
        facing = grad_depth * l0 + grad_rows * l1 + grad_cols * l2
        squared = grad_depth * grad_depth + grad_rows * grad_rows + grad_cols * grad_cols
        return 0.25 + 0.75 * facing * facing / (squared + 1.0)

    def lookup(s):
        scaled = s * 256.0
        floor = jnp.minimum(jnp.floor(scaled), 255.0)
        fraction = scaled - floor
        code = floor.astype(jnp.int32)
        low = code & 127
        second = code > 127
        out = []
        for c in range(4):
            pair = []
            for w in range(2):
                v0 = jnp.take_along_axis(tabs[4 * c + 2 * w], low, axis=1, mode="promise_in_bounds")
                v1 = jnp.take_along_axis(tabs[4 * c + 2 * w + 1], low, axis=1, mode="promise_in_bounds")
                pair.append(jnp.where(second, v1, v0))
            out.append(pair[0] + fraction * pair[1])
        return out

    def brick(src, base, d):
        def row(i, carry):
            def at(k, r):
                return src[k, pl.ds(pl.multiple_of(base + 8 * (i + r), 8), 8), :]

            s0, s1 = at(0, 1), at(1, 1)
            grad_depth = s1 - s0
            sh0 = shade(s0, at(0, 0), at(0, 2), grad_depth)
            sh1 = shade(s1, at(1, 0), at(1, 2), grad_depth)
            v0, v1 = lookup(s0), lookup(s1)
            keep = 1.0 - v0[3]
            w0 = v0[3] * sh0
            w1 = v1[3] * sh1 * keep
            for c in range(3):
                stage[d, i, c] = w0 * v0[c] + w1 * v1[c]
            stage[d, i, 3] = keep * (1.0 - v1[3])
            return carry

        lax.fori_loop(0, ROWS, row, 0)

    def x_copy(d, e):
        number = ((y + GY - d) % GY) * GJ + j
        return remote(stage.at[d, (j + e) % GJ], comp.at[number], xs_sem.at[d, e], xr_sem.at[d, e], x_peer(e))

    def hand_out(d):
        number = ((y + GY - d) % GY) * GJ + j
        for e in range(1, GJ):
            x_copy(d, e).start()
        comp[number] = stage[d, j]

    brick(buf, 64 * y, 0)
    hand_out(0)

    def step(s, carry):
        d = jnp.where(s % 2 == 1, (s + 1) // 2, GY - s // 2)
        y_copy(d).wait_recv()
        brick(recv.at[d], 0, d)
        hand_out(d)
        return carry

    lax.fori_loop(1, GY, step, 0)

    order_copy.wait()

    def settle(d, carry):
        for e in range(1, GJ):
            x_copy(d, e).wait_recv()
        return carry

    lax.fori_loop(0, GY, settle, 0)

    def composite(p, carry):
        red, green, blue, through = carry
        b = ord_s[0, p]
        red = red + comp[b, 0] * through
        green = green + comp[b, 1] * through
        blue = blue + comp[b, 2] * through
        return red, green, blue, through * comp[b, 3]

    zero = jnp.zeros((8, 128), jnp.float32)
    red, green, blue, through = lax.fori_loop(0, 64, composite, (zero, zero, zero, zero + 1.0), unroll=8)
    out_ref[0] = red
    out_ref[1] = green
    out_ref[2] = blue
    out_ref[3] = 1.0 - through

    def drain(d, carry):
        for e in range(1, GJ):
            x_copy(d, e).wait_send()
        return carry

    lax.fori_loop(0, GY, drain, 0)
    for d in range(1, GY):
        y_copy(d).wait_send()

    @pl.when(g < GZ - 1)
    def _():
        down.wait_send()

    @pl.when(g > 0)
    def _():
        up.wait_send()


def shards(scalar, bin_index, color_table, opacity_table, light_dir, view_order):
    table = jnp.concatenate([color_table, opacity_table[None]], axis=0).astype(jnp.float32)
    lower, upper = table[:, :-1], table[:, 1:]
    tables = jnp.stack([lower, upper - lower], axis=1).reshape(16, 128)
    vmem, smem = pl.BlockSpec(memory_space=pltpu.VMEM), pl.BlockSpec(memory_space=pltpu.SMEM)
    f32, dma = jnp.float32, pltpu.SemaphoreType.DMA
    image = pl.pallas_call(
        kernel,
        out_shape=jax.ShapeDtypeStruct((4, 8, 128), f32),
        in_specs=[vmem, vmem, smem, smem],
        out_specs=vmem,
        scratch_shapes=[
            pltpu.VMEM((2, 528, 128), f32),
            pltpu.VMEM((GY, 2, MSG, 128), f32),
            pltpu.VMEM((GY, ROWS, 4, 8, 128), f32),
            pltpu.VMEM((GY * GJ, 4, 8, 128), f32),
            pltpu.VMEM((16, 8, 128), f32),
            pltpu.VMEM((8, 128), jnp.int32),
            pltpu.SMEM((8, 128), jnp.int32),
            dma((GY,)), dma((GY,)), dma((2,)), dma((2,)), dma((GY, GJ)), dma((GY, GJ)), dma,
        ],
        compiler_params=pltpu.CompilerParams(collective_id=0, has_side_effects=True),
    )(scalar, tables, light_dir, view_order)
    return image.reshape(4, 1, 1, 1024)


def solution(mesh):
    in_specs = (P("gz", "gy", None), P("gz", "gy", None), P(), P(), P(), P())
    out_specs = P(None, "gy", "gz", None)
    return jax.shard_map(shards, mesh=mesh, in_specs=in_specs, out_specs=out_specs, check_vma=False)
```

time: 330 us -> 41.9 us (0.13)
  the two profiles are of different devices: /device:TPU:1 before, /device:TPU:321 now
where the time goes in v1:
time: 41.9 us; the launch traced here: 41.7 us
  Pallas kernels  38.3 us (91%)
  local copies, waits for them, and re-layouts  2.63 us (6%)
  other arithmetic  0.77 us (2%)
    pallas_call x1, Pallas kernels, shards(): pl.pallas_call(kernel, out_shape=jax.ShapeDtypeStruct((4, 8, 128), f32),...  38.3 us
    unnamed x1, local copies, waits for them, and re-layouts  1.32 us

profile of v1, /device:TPU:321, one launch (start us, length us, event | category | flops | bytes accessed | tf_op | source)
XLA Modules:
  0.0 41.7 jit_solution(4361369329504742655)
XLA Ops:
  0.0 0.7 %broadcast_in_dim.3 = bf16[1,257]{1,0:T(2,128)(2,1)S(1)} reshape(bf16[257]{0:T(512)(128)(2,1)} %param.8) | data formatting | bytes 1028 | tf_op jit(solution)/shard_map/broadcast_in_dim | solution.py:227
  0.7 0.7 %maximum_convert_fusion = f32[4,257]{1,0:T(4,128)S(1)} fusion(bf16[1,257]{1,0:T(2,128)(2,1)S(1)} %broadcast_in_dim.3, bf16[3,257]{1,0:T(4,128)(2,1)} %param.7), kind=kLoop, calls=%fused_computation.4 | loop fusion | flops 4112 | bytes 6168 | tf_op jit(solution)/shard_map/convert_element_type | solution.py:227
  1.4 0.1 slice_bitcast_fusion
  1.5 0.6 %reshape.6.tab_ref = f32[16,128]{1,0:T(8,128)} reshape(f32[4,2,256]{2,1,0:T(2,128)S(1)} %copy.6) | data formatting | bytes 16384 | tf_op jit(solution)/shard_map/reshape | solution.py:229
  2.1 38.3 %shard_map.55 = f32[4,8,128]{2,1,0:T(8,128)} custom-call(f32[2,64,1024]{2,1,0:T(8,128)} %x_ref.1, f32[16,128]{1,0:T(8,128)} %reshape.6.tab_ref, f32[3]{0:T(128)} %light_ref.1, s32[64]{0:T(128)} %order_ref.1), custom_call_target="tpu_custom_call" | custom-call | tf_op jit(solution)/shard_map/pallas_call | solution.py:232
  40.3 1.3 %copy.9 = f32[4,1,1,1024]{3,2,1,0:T(1,128)} copy(f32[4,1,1,1024]{3,2,1,0:T(1,128)} %bitcast.5) | data formatting | bytes 32768
  (2 shorter events, 0.0 us)

commit v2 on v1

v2 whole, which is shorter than its diff:
```python
import jax
import jax.numpy as jnp
from jax import lax
from jax.experimental import pallas as pl
from jax.experimental.pallas import tpu as pltpu
from jax.sharding import PartitionSpec as P

MESH = pl.DeviceIdType.MESH
GY, GJ, GZ = 8, 8, 8
ROWS = 8
NEAR, FAR = (1, 7, 2, 6), (3, 5, 4)
X_ORDER = (4, 3, 5, 2, 6, 1, 7)


def remote(src, dst, send_sem, recv_sem, device):
    return pltpu.make_async_remote_copy(
        src_ref=src, dst_ref=dst, send_sem=send_sem, recv_sem=recv_sem, device_id=device, device_id_type=MESH
    )


def kernel(
    x_ref, color_hbm, opacity_hbm, light_hbm, order_hbm, out_ref,
    color_ref, opacity_ref, light_ref, order_ref,
    xv, zrow, halo, recv, recv_halo, stage, comp, tabs, ord_v, ord_s,
    in_sem, small_sem, ys_sem, yr_sem, hs_sem, hr_sem, zs_sem, zr_sem, xs_sem, xr_sem, o_sem,
):
    me, g = lax.axis_index("gz"), lax.axis_index("gy")
    y, j = me // GJ, me % GJ

    def y_peer(d):
        return (((y + d) % GY) * GJ + j, g)

    def x_peer(d):
        return (y * GJ + (j + d) % GJ, g)

    barrier = pltpu.get_barrier_semaphore()
    for d in (4, 3, 5, 2, 6, 1, 7):
        pl.semaphore_signal(barrier, inc=1, device_id=y_peer(d), device_id_type=MESH)
        pl.semaphore_signal(barrier, inc=1, device_id=x_peer(d), device_id_type=MESH)

    @pl.when(g > 0)
    def _():
        pl.semaphore_signal(barrier, inc=1, device_id=(me, g - 1), device_id_type=MESH)

    @pl.when(g < GZ - 1)
    def _():
        pl.semaphore_signal(barrier, inc=1, device_id=(me, g + 1), device_id_type=MESH)

    load = pltpu.make_async_copy(x_ref, xv, in_sem)
    load.start()
    small = [
        pltpu.make_async_copy(source, target, small_sem.at[i])
        for i, (source, target) in enumerate(
            ((color_hbm, color_ref), (opacity_hbm, opacity_ref), (light_hbm, light_ref), (order_hbm, order_ref))
        )
    ]
    for copy in small:
        copy.start()

    lane = lax.broadcasted_iota(jnp.int32, (8, 128), 1)
    sub = lax.broadcasted_iota(jnp.int32, (8, 128), 0)

    load.wait()
    for k in range(2):
        zrow[0, k] = xv[k, 63:64, :]
        zrow[1, k] = xv[k, 0:1, :]
        for t in range(8):
            if t > 0:
                halo[t, k] = xv[k, 8 * t - 1 : 8 * t, :]
            if t < 7:
                halo[t, 2 + k] = xv[k, 8 * t + 8 : 8 * t + 9, :]

    @pl.when(g == 0)
    def _():
        halo[0, 0:2] = jnp.zeros((2, 1, 1024), jnp.float32)

    @pl.when(g == GZ - 1)
    def _():
        halo[7, 2:4] = jnp.zeros((2, 1, 1024), jnp.float32)

    def fill(c, values):
        for h in range(2):
            lower, upper = values[:, 128 * h : 128 * h + 128], values[:, 128 * h + 1 : 128 * h + 129]
            tabs[4 * c + h] = jnp.broadcast_to(lower, (8, 128))
            tabs[4 * c + 2 + h] = jnp.broadcast_to(upper - lower, (8, 128))

    for copy in small:
        copy.wait()
    colors = color_ref[...].astype(jnp.float32)
    for c in range(3):
        fill(c, colors[c : c + 1])
    fill(3, opacity_ref[...].astype(jnp.float32).reshape(1, 257))

    pl.semaphore_wait(barrier, 14 + jnp.where(g > 0, 1, 0) + jnp.where(g < GZ - 1, 1, 0))

    down = remote(zrow.at[0], halo.at[0, pl.ds(0, 2)], zs_sem.at[0], zr_sem.at[0], (me, (g + 1) % GZ))
    up = remote(zrow.at[1], halo.at[7, pl.ds(2, 2)], zs_sem.at[1], zr_sem.at[1], (me, (g + GZ - 1) % GZ))

    @pl.when(g < GZ - 1)
    def _():
        down.start()

    @pl.when(g > 0)
    def _():
        up.start()

    def y_copy(d):
        t = (y + d) % GY
        rows = x_ref.at[:, pl.ds(pl.multiple_of(ROWS * t, ROWS), ROWS), :]
        return remote(rows, recv.at[d], ys_sem.at[d], yr_sem.at[d], y_peer(d))

    def halo_copy(d):
        return remote(halo.at[(y + d) % GY], recv_halo.at[d], hs_sem.at[d], hr_sem.at[d], y_peer(d))

    def inner_halo(d):
        t = (y + d) % GY

        @pl.when((t > 0) & (t < GY - 1))
        def _():
            halo_copy(d).start()

    for d in NEAR:
        inner_halo(d)
        y_copy(d).start()

    @pl.when(g > 0)
    def _():
        down.wait_recv()

    @pl.when(g < GZ - 1)
    def _():
        up.wait_recv()

    for d in NEAR + FAR:
        t = (y + d) % GY

        @pl.when((t == 0) | (t == GY - 1))
        def _():
            halo_copy(d).start()

    for d in FAR:
        inner_halo(d)
        y_copy(d).start()

    l0, l1, l2 = light_ref[0], light_ref[1], light_ref[2]

    def lookup(s):
        scaled = s * 256.0
        floor = jnp.minimum(jnp.floor(scaled), 255.0)
        fraction = scaled - floor
        code = floor.astype(jnp.int32)
        low = code & 127
        second = code > 127
        out = []
        for c in range(4):
            pair = []
            for w in range(2):
                v0 = jnp.take_along_axis(tabs[4 * c + 2 * w], low, axis=1, mode="promise_in_bounds")
                v1 = jnp.take_along_axis(tabs[4 * c + 2 * w + 1], low, axis=1, mode="promise_in_bounds")
                pair.append(jnp.where(second, v1, v0))
            out.append(pair[0] + fraction * pair[1])
        return out

    first, last, top, bottom = lane == 0, lane == 127, sub == 0, sub == 7

    def brick(main, edge, d):
        cells = [[main(k, a) for a in range(8)] for k in range(2)]
        after = [[pltpu.roll(cells[k][a], 127, 1) for a in range(8)] for k in range(2)]
        before = [[pltpu.roll(cells[k][a], 1, 1) for a in range(8)] for k in range(2)]
        for a in range(8):
            grad_depth = cells[1][a] - cells[0][a]
            shading, looked = [], []
            for k in range(2):
                s = cells[k][a]
                right = jnp.where(last, after[k][a + 1] if a < 7 else 0.0, after[k][a])
                left = jnp.where(first, before[k][a - 1] if a > 0 else 0.0, before[k][a])
                above = jnp.where(top, jnp.broadcast_to(edge(k, a), (8, 128)), pltpu.roll(s, 1, 0))
                below = jnp.where(bottom, jnp.broadcast_to(edge(2 + k, a), (8, 128)), pltpu.roll(s, 7, 0))
                grad_cols, grad_rows = right - left, below - above
                facing = grad_depth * l0 + grad_rows * l1 + grad_cols * l2
                squared = grad_depth * grad_depth + grad_rows * grad_rows + grad_cols * grad_cols
                shading.append(0.25 + 0.75 * facing * facing / (squared + 1.0))
                looked.append(lookup(s))
            v0, v1 = looked
            keep = 1.0 - v0[3]
            w0 = v0[3] * shading[0]
            w1 = v1[3] * shading[1] * keep
            for c in range(3):
                stage[d, pl.ds(8 * c + a, 8, stride=32), :] = w0 * v0[c] + w1 * v1[c]
            stage[d, pl.ds(24 + a, 8, stride=32), :] = keep * (1.0 - v1[3])

    def x_copy(d, e):
        number = ((y + GY - d) % GY) * GJ + j
        rows = stage.at[d, pl.ds(pl.multiple_of(32 * ((j + e) % GJ), 32), 32)]
        return remote(rows, comp.at[number], xs_sem.at[d, e], xr_sem.at[d, e], x_peer(e))

    def hand_out(d):
        number = ((y + GY - d) % GY) * GJ + j
        for e in X_ORDER:
            x_copy(d, e).start()
        comp[number] = stage[d, pl.ds(pl.multiple_of(32 * j, 32), 32)]

    def column(a):
        return slice(128 * a, 128 * a + 128)

    own = pl.ds(pl.multiple_of(ROWS * y, ROWS), ROWS)
    brick(lambda k, a: xv[k, own, column(a)], lambda r, a: halo[y, r, :, column(a)], 0)
    hand_out(0)

    inverse = jnp.zeros((8, 128), jnp.int32)
    for b in range(64):
        inverse = jnp.where(lane == order_ref[b], b, inverse)
    ord_v[...] = inverse
    order_copy = pltpu.make_async_copy(ord_v, ord_s, o_sem)
    order_copy.start()

    def step(s, carry):
        d = jnp.where(s % 2 == 1, (s + 1) // 2, GY - s // 2)
        halo_copy(d).wait_recv()
        y_copy(d).wait_recv()
        brick(lambda k, a: recv[d, k, :, column(a)], lambda r, a: recv_halo[d, r, :, column(a)], d)
        hand_out(d)
        return carry

    lax.fori_loop(1, GY, step, 0)

    order_copy.wait()

    def settle(d, carry):
        for e in X_ORDER:
            x_copy(d, e).wait_recv()
        return carry

    lax.fori_loop(0, GY, settle, 0)

    def composite(p, carry):
        red, green, blue, through = carry
        b = ord_s[0, p]
        red = red + comp[b, 0:8] * through
        green = green + comp[b, 8:16] * through
        blue = blue + comp[b, 16:24] * through
        return red, green, blue, through * comp[b, 24:32]

    zero = jnp.zeros((8, 128), jnp.float32)
    red, green, blue, through = lax.fori_loop(0, 64, composite, (zero, zero, zero, zero + 1.0), unroll=8)
    out_ref[0] = red
    out_ref[1] = green
    out_ref[2] = blue
    out_ref[3] = 1.0 - through

    def drain(d, carry):
        for e in X_ORDER:
            x_copy(d, e).wait_send()
        return carry

    lax.fori_loop(0, GY, drain, 0)
    for d in range(1, GY):
        y_copy(d).wait_send()
        halo_copy(d).wait_send()

    @pl.when(g < GZ - 1)
    def _():
        down.wait_send()

    @pl.when(g > 0)
    def _():
        up.wait_send()


def shards(scalar, bin_index, color_table, opacity_table, light_dir, view_order):
    f32, dma = jnp.float32, pltpu.SemaphoreType.DMA
    image = pl.pallas_call(
        kernel,
        out_shape=jax.ShapeDtypeStruct((4, 8, 128), f32),
        in_specs=[pl.BlockSpec(memory_space=pltpu.HBM)] * 5,
        out_specs=pl.BlockSpec(memory_space=pltpu.VMEM),
        scratch_shapes=[
            pltpu.VMEM(color_table.shape, color_table.dtype),
            pltpu.VMEM(opacity_table.shape, opacity_table.dtype),
            pltpu.SMEM(light_dir.shape, light_dir.dtype),
            pltpu.SMEM(view_order.shape, view_order.dtype),
            pltpu.VMEM((2, 64, 1024), f32),
            pltpu.VMEM((2, 2, 1, 1024), f32),
            pltpu.VMEM((GY, 4, 1, 1024), f32),
            pltpu.VMEM((GY, 2, ROWS, 1024), f32),
            pltpu.VMEM((GY, 4, 1, 1024), f32),
            pltpu.VMEM((GY, ROWS * 32, 128), f32),
            pltpu.VMEM((GY * GJ, 32, 128), f32),
            pltpu.VMEM((16, 8, 128), f32),
            pltpu.VMEM((8, 128), jnp.int32),
            pltpu.SMEM((8, 128), jnp.int32),
            dma, dma((4,)), dma((GY,)), dma((GY,)), dma((GY,)), dma((GY,)), dma((2,)), dma((2,)), dma((GY, GJ)), dma((GY, GJ)), dma,
        ],
        compiler_params=pltpu.CompilerParams(collective_id=0, has_side_effects=True),
    )(scalar, color_table, opacity_table, light_dir, view_order)
    return image.reshape(4, 1, 1, 1024)


def solution(mesh):
    in_specs = (P("gz", "gy", None), P("gz", "gy", None), P(), P(), P(), P())
    out_specs = P(None, "gy", "gz", None)
    return jax.shard_map(shards, mesh=mesh, in_specs=in_specs, out_specs=out_specs, check_vma=False)
```

time: 41.9 us -> 34.3 us (0.82)
  the two profiles are of different devices: /device:TPU:321 before, /device:TPU:1 now
where the time goes in v2:
time: 34.3 us; the launch traced here: 33.7 us
  Pallas kernels  32.4 us (94%)
  local copies, waits for them, and re-layouts  1.32 us (4%)
    pallas_call x1, Pallas kernels, shards(): pl.pallas_call(kernel, out_shape=jax.ShapeDtypeStruct((4, 8, 128), f32),...  32.4 us
    unnamed x1, local copies, waits for them, and re-layouts  1.32 us

profile of v2, /device:TPU:1, one launch (start us, length us, event | category | flops | bytes accessed | tf_op | source)
XLA Modules:
  0.0 33.7 jit_solution(12531112827094941624)
XLA Ops:
  0.0 32.4 %shard_map.55 = f32[4,8,128]{2,1,0:T(8,128)} custom-call(f32[2,64,1024]{2,1,0:T(8,128)} %x_ref.1, bf16[3,257]{1,0:T(4,128)(2,1)} %color_hbm.1, bf16[257]{0:T(512)(128)(2,1)} %opacity_hbm.1, f32[3]{0:T(128)} %light_hbm.1, s32[64]{0:T(128)} %order_hbm.1), custom_call_target="tpu_custom_call" | custom-call | tf_op jit(solution)/shard_map/pallas_call | solution.py:272
  32.4 1.3 %copy.8 = f32[4,1,1,1024]{3,2,1,0:T(1,128)} copy(f32[4,1,1,1024]{3,2,1,0:T(1,128)} %bitcast.1) | data formatting | bytes 32768

commit v3 on v2

--- a/solution.py
+++ b/solution.py
@@ -22,7 +22,7 @@
     x_ref, color_hbm, opacity_hbm, light_hbm, order_hbm, out_ref,
     color_ref, opacity_ref, light_ref, order_ref,
     xv, zrow, halo, recv, recv_halo, stage, comp, tabs, ord_v, ord_s,
-    in_sem, small_sem, ys_sem, yr_sem, hs_sem, hr_sem, zs_sem, zr_sem, xs_sem, xr_sem, o_sem,
+    in_sem, small_sem, ys_sem, yr_sem, hs_sem, hr_sem, zs_sem, zr_sem, xs_sem, xr_sem, o_sem, beyond_sem,
 ):
     me, g = lax.axis_index("gz"), lax.axis_index("gy")
     y, j = me // GJ, me % GJ
@@ -34,9 +34,8 @@
         return (y * GJ + (j + d) % GJ, g)
 
     barrier = pltpu.get_barrier_semaphore()
-    for d in (4, 3, 5, 2, 6, 1, 7):
-        pl.semaphore_signal(barrier, inc=1, device_id=y_peer(d), device_id_type=MESH)
-        pl.semaphore_signal(barrier, inc=1, device_id=x_peer(d), device_id_type=MESH)
+    for device in [x_peer(d) for d in X_ORDER] + [y_peer(d) for d in (2, 6, 1, 7)]:
+        pl.semaphore_signal(barrier, inc=1, device_id=device, device_id_type=MESH)
 
     @pl.when(g > 0)
     def _():
@@ -60,10 +59,44 @@
     lane = lax.broadcasted_iota(jnp.int32, (8, 128), 1)
     sub = lax.broadcasted_iota(jnp.int32, (8, 128), 0)
 
+    def y_copy(d):
+        t = (y + d) % GY
+        rows = x_ref.at[:, pl.ds(pl.multiple_of(ROWS * t, ROWS), ROWS), :]
+        return remote(rows, recv.at[d], ys_sem, yr_sem.at[d], y_peer(d))
+
+    def halo_copy(d):
+        return remote(halo.at[(y + d) % GY], recv_halo.at[d], hs_sem, hr_sem.at[d], y_peer(d))
+
+    def inner_halo(d):
+        t = (y + d) % GY
+
+        @pl.when((t > 0) & (t < GY - 1))
+        def _():
+            halo_copy(d).start()
+
+    pl.semaphore_wait(barrier, 11 + jnp.where(g > 0, 1, 0) + jnp.where(g < GZ - 1, 1, 0))
+    pl.semaphore_signal(beyond_sem, inc=1, device_id=y_peer(2), device_id_type=MESH)
+    pl.semaphore_signal(beyond_sem, inc=1, device_id=y_peer(6), device_id_type=MESH)
+    y_copy(1).start()
+    y_copy(7).start()
+
     load.wait()
     for k in range(2):
         zrow[0, k] = xv[k, 63:64, :]
         zrow[1, k] = xv[k, 0:1, :]
+
+    down = remote(zrow.at[0], halo.at[0, pl.ds(0, 2)], zs_sem.at[0], zr_sem.at[0], (me, (g + 1) % GZ))
+    up = remote(zrow.at[1], halo.at[7, pl.ds(2, 2)], zs_sem.at[1], zr_sem.at[1], (me, (g + GZ - 1) % GZ))
+
+    @pl.when(g < GZ - 1)
+    def _():
+        down.start()
+
+    @pl.when(g > 0)
+    def _():
+        up.start()
+
+    for k in range(2):
         for t in range(8):
             if t > 0:
                 halo[t, k] = xv[k, 8 * t - 1 : 8 * t, :]
@@ -77,6 +110,12 @@
     @pl.when(g == GZ - 1)
     def _():
         halo[7, 2:4] = jnp.zeros((2, 1, 1024), jnp.float32)
+
+    inner_halo(1)
+    inner_halo(7)
+    for d in (2, 6):
+        inner_halo(d)
+        y_copy(d).start()
 
     def fill(c, values):
         for h in range(2):
@@ -90,57 +129,6 @@
     for c in range(3):
         fill(c, colors[c : c + 1])
     fill(3, opacity_ref[...].astype(jnp.float32).reshape(1, 257))
-
-    pl.semaphore_wait(barrier, 14 + jnp.where(g > 0, 1, 0) + jnp.where(g < GZ - 1, 1, 0))
-
-    down = remote(zrow.at[0], halo.at[0, pl.ds(0, 2)], zs_sem.at[0], zr_sem.at[0], (me, (g + 1) % GZ))
-    up = remote(zrow.at[1], halo.at[7, pl.ds(2, 2)], zs_sem.at[1], zr_sem.at[1], (me, (g + GZ - 1) % GZ))
-
-    @pl.when(g < GZ - 1)
-    def _():
-        down.start()
-
-    @pl.when(g > 0)
-    def _():
-        up.start()
-
-    def y_copy(d):
-        t = (y + d) % GY
-        rows = x_ref.at[:, pl.ds(pl.multiple_of(ROWS * t, ROWS), ROWS), :]
-        return remote(rows, recv.at[d], ys_sem.at[d], yr_sem.at[d], y_peer(d))
-
-    def halo_copy(d):
-        return remote(halo.at[(y + d) % GY], recv_halo.at[d], hs_sem.at[d], hr_sem.at[d], y_peer(d))
-
-    def inner_halo(d):
-        t = (y + d) % GY
-
-        @pl.when((t > 0) & (t < GY - 1))
-        def _():
-            halo_copy(d).start()
-
-    for d in NEAR:
-        inner_halo(d)
-        y_copy(d).start()
-
-    @pl.when(g > 0)
-    def _():
-        down.wait_recv()
-
-    @pl.when(g < GZ - 1)
-    def _():
-        up.wait_recv()
-
-    for d in NEAR + FAR:
-        t = (y + d) % GY
-
-        @pl.when((t == 0) | (t == GY - 1))
-        def _():
-            halo_copy(d).start()
-
-    for d in FAR:
-        inner_halo(d)
-        y_copy(d).start()
 
     l0, l1, l2 = light_ref[0], light_ref[1], light_ref[2]
 
@@ -192,7 +180,7 @@
     def x_copy(d, e):
         number = ((y + GY - d) % GY) * GJ + j
         rows = stage.at[d, pl.ds(pl.multiple_of(32 * ((j + e) % GJ), 32), 32)]
-        return remote(rows, comp.at[number], xs_sem.at[d, e], xr_sem.at[d, e], x_peer(e))
+        return remote(rows, comp.at[number], xs_sem, xr_sem, x_peer(e))
 
     def hand_out(d):
         number = ((y + GY - d) % GY) * GJ + j
@@ -204,7 +192,39 @@
         return slice(128 * a, 128 * a + 128)
 
     own = pl.ds(pl.multiple_of(ROWS * y, ROWS), ROWS)
+
+    def band_halos():
+        @pl.when(g > 0)
+        def _():
+            down.wait_recv()
+
+        @pl.when(g < GZ - 1)
+        def _():
+            up.wait_recv()
+
+    edge = (y == 0) | (y == GY - 1)
+
+    @pl.when(edge)
+    def _():
+        band_halos()
+
     brick(lambda k, a: xv[k, own, column(a)], lambda r, a: halo[y, r, :, column(a)], 0)
+    pl.semaphore_wait(beyond_sem, 2)
+
+    @pl.when(jnp.logical_not(edge))
+    def _():
+        band_halos()
+
+    for d in NEAR + FAR:
+        t = (y + d) % GY
+
+        @pl.when((t == 0) | (t == GY - 1))
+        def _():
+            halo_copy(d).start()
+
+    for d in FAR:
+        inner_halo(d)
+        y_copy(d).start()
     hand_out(0)
 
     inverse = jnp.zeros((8, 128), jnp.int32)
@@ -226,12 +246,8 @@
 
     order_copy.wait()
 
-    def settle(d, carry):
-        for e in X_ORDER:
-            x_copy(d, e).wait_recv()
-        return carry
-
-    lax.fori_loop(0, GY, settle, 0)
+    bricks = comp.at[pl.ds(0, 56)]
+    pltpu.make_async_copy(bricks, bricks, xr_sem).wait()
 
     def composite(p, carry):
         red, green, blue, through = carry
@@ -248,15 +264,9 @@
     out_ref[2] = blue
     out_ref[3] = 1.0 - through
 
-    def drain(d, carry):
-        for e in X_ORDER:
-            x_copy(d, e).wait_send()
-        return carry
-
-    lax.fori_loop(0, GY, drain, 0)
-    for d in range(1, GY):
-        y_copy(d).wait_send()
-        halo_copy(d).wait_send()
+    for buffer, semaphore in ((stage, xs_sem), (recv, ys_sem), (recv_halo, hs_sem)):
+        sent = buffer.at[pl.ds(0, 7)]
+        pltpu.make_async_copy(sent, sent, semaphore).wait()
 
     @pl.when(g < GZ - 1)
     def _():
@@ -271,7 +281,7 @@
     f32, dma = jnp.float32, pltpu.SemaphoreType.DMA
     image = pl.pallas_call(
         kernel,
-        out_shape=jax.ShapeDtypeStruct((4, 8, 128), f32),
+        out_shape=pltpu.VMEM((4, 8, 128), f32),
         in_specs=[pl.BlockSpec(memory_space=pltpu.HBM)] * 5,
         out_specs=pl.BlockSpec(memory_space=pltpu.VMEM),
         scratch_shapes=[
@@ -289,7 +299,7 @@
             pltpu.VMEM((16, 8, 128), f32),
             pltpu.VMEM((8, 128), jnp.int32),
             pltpu.SMEM((8, 128), jnp.int32),
-            dma, dma((4,)), dma((GY,)), dma((GY,)), dma((GY,)), dma((GY,)), dma((2,)), dma((2,)), dma((GY, GJ)), dma((GY, GJ)), dma,
+            dma, dma((4,)), dma, dma((GY,)), dma, dma((GY,)), dma((2,)), dma((2,)), dma, dma, dma, pltpu.SemaphoreType.REGULAR,
         ],
         compiler_params=pltpu.CompilerParams(collective_id=0, has_side_effects=True),
     )(scalar, color_table, opacity_table, light_dir, view_order)

time: 34.3 us -> 31.6 us (0.921)
  Pallas kernels: 32.4 us -> 30.5 us
  local copies, waits for them, and re-layouts: 1.32 us -> 0.61 us
    pallas_call x1, Pallas kernels: 32.4 us -> 30.5 us  [shards(): pl.pallas_call(kernel, out_shape=pltpu.VMEM((4, 8, 128), f32), in_specs=[...]
    unnamed x1, local copies, waits for them, and re-layouts: 1.32 us -> 0.61 us
where the time goes in v3:
time: 31.6 us; the launch traced here: 31.1 us
  Pallas kernels  30.5 us (97%)
  local copies, waits for them, and re-layouts  0.61 us (2%)
    pallas_call x1, Pallas kernels, shards(): pl.pallas_call(kernel, out_shape=pltpu.VMEM((4, 8, 128), f32), in_specs=[...  30.5 us

profile of v3, /device:TPU:1, one launch (start us, length us, event | category | flops | bytes accessed | tf_op | source)
XLA Modules:
  0.0 31.1 jit_solution(12458481040725154736)
XLA Ops:
  0.0 30.5 %shard_map.55 = f32[4,8,128]{2,1,0:T(8,128)S(1)} custom-call(f32[2,64,1024]{2,1,0:T(8,128)} %x_ref.1, bf16[3,257]{1,0:T(4,128)(2,1)} %color_hbm.1, bf16[257]{0:T(512)(128)(2,1)} %opacity_hbm.1, f32[3]{0:T(128)} %light_hbm.1, s32[64]{0:T(128)} %order_hbm.1), custom_call_target="tpu_custom_call" | custom-call | tf_op jit(solution)/shard_map/pallas_call | solution.py:282
  30.5 0.6 %copy.8 = f32[4,1,1,1024]{3,2,1,0:T(1,128)} copy(f32[4,1,1,1024]{3,2,1,0:T(1,128)S(1)} %bitcast.1) | data formatting | bytes 32768

commit v4 on v3

--- a/solution.py
+++ b/solution.py
@@ -22,7 +22,7 @@
     x_ref, color_hbm, opacity_hbm, light_hbm, order_hbm, out_ref,
     color_ref, opacity_ref, light_ref, order_ref,
     xv, zrow, halo, recv, recv_halo, stage, comp, tabs, ord_v, ord_s,
-    in_sem, small_sem, ys_sem, yr_sem, hs_sem, hr_sem, zs_sem, zr_sem, xs_sem, xr_sem, o_sem, beyond_sem,
+    in_sem, small_sem, ys_sem, yr_sem, hs_sem, hr_sem, zs_sem, zr_sem, xs_sem, xr_sem, o_sem, beyond_sem, band_sem,
 ):
     me, g = lax.axis_index("gz"), lax.axis_index("gy")
     y, j = me // GJ, me % GJ
@@ -36,10 +36,6 @@
     barrier = pltpu.get_barrier_semaphore()
     for device in [x_peer(d) for d in X_ORDER] + [y_peer(d) for d in (2, 6, 1, 7)]:
         pl.semaphore_signal(barrier, inc=1, device_id=device, device_id_type=MESH)
-
-    @pl.when(g > 0)
-    def _():
-        pl.semaphore_signal(barrier, inc=1, device_id=(me, g - 1), device_id_type=MESH)
 
     @pl.when(g < GZ - 1)
     def _():
@@ -74,12 +70,16 @@
         def _():
             halo_copy(d).start()
 
-    pl.semaphore_wait(barrier, 11 + jnp.where(g > 0, 1, 0) + jnp.where(g < GZ - 1, 1, 0))
+    pl.semaphore_wait(barrier, 11 + jnp.where(g > 0, 1, 0))
     pl.semaphore_signal(beyond_sem, inc=1, device_id=y_peer(2), device_id_type=MESH)
     pl.semaphore_signal(beyond_sem, inc=1, device_id=y_peer(6), device_id_type=MESH)
     y_copy(1).start()
     y_copy(7).start()
 
+    @pl.when(g > 0)
+    def _():
+        pl.semaphore_signal(band_sem, inc=1, device_id=(me, g - 1), device_id_type=MESH)
+
     load.wait()
     for k in range(2):
         zrow[0, k] = xv[k, 63:64, :]
@@ -87,10 +87,6 @@
 
     down = remote(zrow.at[0], halo.at[0, pl.ds(0, 2)], zs_sem.at[0], zr_sem.at[0], (me, (g + 1) % GZ))
     up = remote(zrow.at[1], halo.at[7, pl.ds(2, 2)], zs_sem.at[1], zr_sem.at[1], (me, (g + GZ - 1) % GZ))
-
-    @pl.when(g < GZ - 1)
-    def _():
-        down.start()
 
     @pl.when(g > 0)
     def _():
@@ -194,6 +190,11 @@
     own = pl.ds(pl.multiple_of(ROWS * y, ROWS), ROWS)
 
     def band_halos():
+        @pl.when(g < GZ - 1)
+        def _():
+            pl.semaphore_wait(band_sem, 1)
+            down.start()
+
         @pl.when(g > 0)
         def _():
             down.wait_recv()
@@ -209,6 +210,7 @@
         band_halos()
 
     brick(lambda k, a: xv[k, own, column(a)], lambda r, a: halo[y, r, :, column(a)], 0)
+    hand_out(0)
     pl.semaphore_wait(beyond_sem, 2)
 
     @pl.when(jnp.logical_not(edge))
@@ -225,7 +227,6 @@
     for d in FAR:
         inner_halo(d)
         y_copy(d).start()
-    hand_out(0)
 
     inverse = jnp.zeros((8, 128), jnp.int32)
     for b in range(64):
@@ -300,6 +301,7 @@
             pltpu.VMEM((8, 128), jnp.int32),
             pltpu.SMEM((8, 128), jnp.int32),
             dma, dma((4,)), dma, dma((GY,)), dma, dma((GY,)), dma((2,)), dma((2,)), dma, dma, dma, pltpu.SemaphoreType.REGULAR,
+            pltpu.SemaphoreType.REGULAR,
         ],
         compiler_params=pltpu.CompilerParams(collective_id=0, has_side_effects=True),
     )(scalar, color_table, opacity_table, light_dir, view_order)

time: 31.6 us -> 30.4 us (0.962); the launches traced: 31.1 us -> 30.3 us
  Pallas kernels: 30.5 us -> 29.6 us
    pallas_call x1, Pallas kernels: 30.5 us -> 29.6 us  [shards(): pl.pallas_call(kernel, out_shape=pltpu.VMEM((4, 8, 128), f32), in_specs=[...]
where the time goes in v4:
time: 30.4 us; the launch traced here: 30.3 us
  Pallas kernels  29.6 us (97%)
  local copies, waits for them, and re-layouts  0.61 us (2%)
    pallas_call x1, Pallas kernels, shards(): pl.pallas_call(kernel, out_shape=pltpu.VMEM((4, 8, 128), f32), in_specs=[...  29.6 us

profile of v4, /device:TPU:1, one launch (start us, length us, event | category | flops | bytes accessed | tf_op | source)
XLA Modules:
  0.0 30.3 jit_solution(385968112477419404)
XLA Ops:
  0.0 29.6 %shard_map.55 = f32[4,8,128]{2,1,0:T(8,128)S(1)} custom-call(f32[2,64,1024]{2,1,0:T(8,128)} %x_ref.1, bf16[3,257]{1,0:T(4,128)(2,1)} %color_hbm.1, bf16[257]{0:T(512)(128)(2,1)} %opacity_hbm.1, f32[3]{0:T(128)} %light_hbm.1, s32[64]{0:T(128)} %order_hbm.1), custom_call_target="tpu_custom_call" | custom-call | tf_op jit(solution)/shard_map/pallas_call | solution.py:283
  29.6 0.6 %copy.8 = f32[4,1,1,1024]{3,2,1,0:T(1,128)} copy(f32[4,1,1,1024]{3,2,1,0:T(1,128)S(1)} %bitcast.1) | data formatting | bytes 32768

commit v5 on v4

--- a/solution.py
+++ b/solution.py
@@ -22,7 +22,7 @@
     x_ref, color_hbm, opacity_hbm, light_hbm, order_hbm, out_ref,
     color_ref, opacity_ref, light_ref, order_ref,
     xv, zrow, halo, recv, recv_halo, stage, comp, tabs, ord_v, ord_s,
-    in_sem, small_sem, ys_sem, yr_sem, hs_sem, hr_sem, zs_sem, zr_sem, xs_sem, xr_sem, o_sem, beyond_sem, band_sem,
+    in_sem, small_sem, ys_sem, yr_sem, hs_sem, hr_sem, zs_sem, zr_sem, xs_sem, xr_sem, o_sem, second_sem, beyond_sem, beside_sem, across_sem, band_sem,
 ):
     me, g = lax.axis_index("gz"), lax.axis_index("gy")
     y, j = me // GJ, me % GJ
@@ -34,7 +34,9 @@
         return (y * GJ + (j + d) % GJ, g)
 
     barrier = pltpu.get_barrier_semaphore()
-    for device in [x_peer(d) for d in X_ORDER] + [y_peer(d) for d in (2, 6, 1, 7)]:
+    partner = (me + 1 - 2 * (j % 2), g)
+    beside = [x_peer(2), x_peer(6), partner]
+    for device in [y_peer(1), y_peer(7)] + beside:
         pl.semaphore_signal(barrier, inc=1, device_id=device, device_id_type=MESH)
 
     @pl.when(g < GZ - 1)
@@ -57,7 +59,7 @@
 
     def y_copy(d):
         t = (y + d) % GY
-        rows = x_ref.at[:, pl.ds(pl.multiple_of(ROWS * t, ROWS), ROWS), :]
+        rows = xv.at[:, pl.ds(pl.multiple_of(ROWS * t, ROWS), ROWS), :]
         return remote(rows, recv.at[d], ys_sem, yr_sem.at[d], y_peer(d))
 
     def halo_copy(d):
@@ -70,9 +72,14 @@
         def _():
             halo_copy(d).start()
 
-    pl.semaphore_wait(barrier, 11 + jnp.where(g > 0, 1, 0))
-    pl.semaphore_signal(beyond_sem, inc=1, device_id=y_peer(2), device_id_type=MESH)
-    pl.semaphore_signal(beyond_sem, inc=1, device_id=y_peer(6), device_id_type=MESH)
+    load.wait()
+    pl.semaphore_wait(barrier, 5 + jnp.where(g > 0, 1, 0))
+    def tell(semaphore, devices):
+        for device in devices:
+            pl.semaphore_signal(semaphore, inc=1, device_id=device, device_id_type=MESH)
+
+    tell(second_sem, [y_peer(1), y_peer(7)])
+    tell(beside_sem, beside)
     y_copy(1).start()
     y_copy(7).start()
 
@@ -80,7 +87,6 @@
     def _():
         pl.semaphore_signal(band_sem, inc=1, device_id=(me, g - 1), device_id_type=MESH)
 
-    load.wait()
     for k in range(2):
         zrow[0, k] = xv[k, 63:64, :]
         zrow[1, k] = xv[k, 0:1, :]
@@ -109,9 +115,13 @@
 
     inner_halo(1)
     inner_halo(7)
+    pl.semaphore_wait(second_sem, 2)
+    tell(beyond_sem, [y_peer(2), y_peer(6)])
     for d in (2, 6):
         inner_halo(d)
         y_copy(d).start()
+    pl.semaphore_wait(beside_sem, 3)
+    tell(across_sem, [partner])
 
     def fill(c, values):
         for h in range(2):
@@ -210,6 +220,7 @@
         band_halos()
 
     brick(lambda k, a: xv[k, own, column(a)], lambda r, a: halo[y, r, :, column(a)], 0)
+    pl.semaphore_wait(across_sem, 1)
     hand_out(0)
     pl.semaphore_wait(beyond_sem, 2)
 
@@ -301,6 +312,7 @@
             pltpu.VMEM((8, 128), jnp.int32),
             pltpu.SMEM((8, 128), jnp.int32),
             dma, dma((4,)), dma, dma((GY,)), dma, dma((GY,)), dma((2,)), dma((2,)), dma, dma, dma, pltpu.SemaphoreType.REGULAR,
+            pltpu.SemaphoreType.REGULAR, pltpu.SemaphoreType.REGULAR, pltpu.SemaphoreType.REGULAR,
             pltpu.SemaphoreType.REGULAR,
         ],
         compiler_params=pltpu.CompilerParams(collective_id=0, has_side_effects=True),

time: 30.4 us -> 29.6 us (0.974)
  Pallas kernels: 29.6 us -> 28.9 us
    pallas_call x1, Pallas kernels: 29.6 us -> 28.9 us  [shards(): pl.pallas_call(kernel, out_shape=pltpu.VMEM((4, 8, 128), f32), in_specs=[...]
where the time goes in v5:
time: 29.6 us; the launch traced here: 29.5 us
  Pallas kernels  28.9 us (98%)
  local copies, waits for them, and re-layouts  0.61 us (2%)
    pallas_call x1, Pallas kernels, shards(): pl.pallas_call(kernel, out_shape=pltpu.VMEM((4, 8, 128), f32), in_specs=[...  28.9 us
    unnamed x1, local copies, waits for them, and re-layouts  0.61 us

profile of v5, /device:TPU:1, one launch (start us, length us, event | category | flops | bytes accessed | tf_op | source)
XLA Modules:
  0.0 29.5 jit_solution(7344899959699257180)
XLA Ops:
  0.0 28.9 %shard_map.55 = f32[4,8,128]{2,1,0:T(8,128)S(1)} custom-call(f32[2,64,1024]{2,1,0:T(8,128)} %x_ref.1, bf16[3,257]{1,0:T(4,128)(2,1)} %color_hbm.1, bf16[257]{0:T(512)(128)(2,1)} %opacity_hbm.1, f32[3]{0:T(128)} %light_hbm.1, s32[64]{0:T(128)} %order_hbm.1), custom_call_target="tpu_custom_call" | custom-call | tf_op jit(solution)/shard_map/pallas_call | solution.py:294
  28.9 0.6 %copy.8 = f32[4,1,1,1024]{3,2,1,0:T(1,128)} copy(f32[4,1,1,1024]{3,2,1,0:T(1,128)S(1)} %bitcast.1) | data formatting | bytes 32768

commit v6 on v5

--- a/solution.py
+++ b/solution.py
@@ -235,7 +235,8 @@
         def _():
             halo_copy(d).start()
 
-    for d in FAR:
+    for a, b in zip((3, 5, 4), (3, 4, 5)):
+        d = jnp.where(j % 2 == 0, a, b)
         inner_halo(d)
         y_copy(d).start()
 

time: 29.6 us -> 29.6 us (level)
  no operation moved by 1% of the time
where the time goes in v6:
time: 29.6 us; the launch traced here: 29.5 us
  Pallas kernels  28.9 us (98%)
  local copies, waits for them, and re-layouts  0.61 us (2%)
    pallas_call x1, Pallas kernels, shards(): pl.pallas_call(kernel, out_shape=pltpu.VMEM((4, 8, 128), f32), in_specs=[...  28.9 us
    unnamed x1, local copies, waits for them, and re-layouts  0.61 us

profile of v6, /device:TPU:1, one launch (start us, length us, event | category | flops | bytes accessed | tf_op | source)
XLA Modules:
  0.0 29.5 jit_solution(13199119478748659057)
XLA Ops:
  0.0 28.9 %shard_map.55 = f32[4,8,128]{2,1,0:T(8,128)S(1)} custom-call(f32[2,64,1024]{2,1,0:T(8,128)} %x_ref.1, bf16[3,257]{1,0:T(4,128)(2,1)} %color_hbm.1, bf16[257]{0:T(512)(128)(2,1)} %opacity_hbm.1, f32[3]{0:T(128)} %light_hbm.1, s32[64]{0:T(128)} %order_hbm.1), custom_call_target="tpu_custom_call" | custom-call | tf_op jit(solution)/shard_map/pallas_call | solution.py:295
  28.9 0.6 %copy.8 = f32[4,1,1,1024]{3,2,1,0:T(1,128)} copy(f32[4,1,1,1024]{3,2,1,0:T(1,128)S(1)} %bitcast.1) | data formatting | bytes 32768
